TPU v7x, 32 devices: a whole 2x2x4 slice. The times are simulated.
32 devices in a mesh: slab: 2 (over x), gal: 4 (over y, core), qb: 4 (over z).
Axes of the slice: x: 2, y: 2, z: 4, core: 2. Of those that a mesh axis runs over, the one named last changes fastest.
Arguments:
- gallery: bfloat16 [16384, 768], P(('slab', 'gal')), parts along dimension 0, may hold values from -512 to 512
- querybank: bfloat16 [8, 2048, 768], P(('slab', 'qb'), 'gal'), parts along dimension 0, may hold values from -512 to 512
- test_queries: bfloat16 [8, 512, 768], P(('slab', 'qb'), 'gal'), parts along dimension 0, may hold values from -512 to 512
Outputs:
- logprob: float32 [4096, 8192], P(('slab', 'qb'), 'gal'), parts along dimension 0
- normalizer: float32 [16384], P(('slab', 'gal')), parts along dimension 0
There are 2 independent parts, one for each index of `slab`. A program takes and returns all parts, laid end to end along the dimension named above; each array names one. Nothing has to cross between parts.
All inputs are finite; a program needn't handle non-finite values.
Results may differ from a plain program's by a relative error of at most 0.00049.
Values may be sent and summed in bfloat16 or wider, within the bound.
No kernel may reach another device: no remote copies, remote signals or barrier semaphores. Data moves between devices by JAX's collectives and lax.ppermute only.
A program may use at most 64 MiB of HBM per device.

v0:
```python
import math
import jax
import jax.numpy as jnp
from jax import lax
from jax.sharding import PartitionSpec as P

sharpness = 20.0


def unit_rows(values):
    wide = values.astype(jnp.float32)
    scaled = wide * lax.rsqrt(jnp.sum(wide * wide, axis=-1, keepdims=True) + 1e-06)
    return scaled.astype(jnp.bfloat16)


def column_terms(bank_block, gallery_unit):
    scores = lax.dot_general(
        bank_block, gallery_unit, (((1,), (1,)), ((), ())), preferred_element_type=jnp.float32
    )
    return jnp.sum(jnp.exp(sharpness * (scores - 1.0)), axis=0)


def bank_columns(bank_block, gallery_unit):
    rows = bank_block.shape[0]
    height = math.gcd(rows, 512)

    def add_block(index, running):
        piece = lax.dynamic_slice_in_dim(bank_block, index * height, height, 0)
        return running + column_terms(piece, gallery_unit)

    initial = jnp.zeros((gallery_unit.shape[0],), jnp.float32)
    return lax.fori_loop(0, rows // height, add_block, initial)


def per_device(gallery, querybank, test_queries):
    gallery_unit = unit_rows(gallery)
    bank_local = unit_rows(querybank[0])
    test_local = unit_rows(test_queries[0])
    bank_all = lax.all_gather(bank_local, "gal", axis=0, tiled=True)
    column_part = bank_columns(bank_all, gallery_unit)
    test_all = lax.all_gather(test_local, "gal", axis=0, tiled=True)
    column_total = lax.psum(column_part, "qb")
    normalizer = sharpness + jnp.log(column_total)
    bank_count = querybank.shape[1] * lax.axis_size("gal") * lax.axis_size("qb")
    offset = 2.0 * sharpness - math.log(bank_count)
    scores = lax.dot_general(
        test_all, gallery_unit, (((1,), (1,)), ((), ())), preferred_element_type=jnp.float32
    )
    logits = sharpness * scores - normalizer[None, :] - offset
    row_part = jnp.sum(jnp.exp(logits), axis=1)
    row_total = lax.psum(row_part, "gal")
    logprob = logits - jnp.log(row_total)[:, None]
    return (logprob, normalizer)


def solution(mesh):
    placed = (
        P(("slab", "gal"), None),
        P(("slab", "qb"), "gal", None),
        P(("slab", "qb"), "gal", None),
    )
    return jax.shard_map(
        per_device,
        mesh=mesh,
        in_specs=placed,
        out_specs=(P(("slab", "qb"), "gal"), P(("slab", "gal"))),
        check_vma=False,
    )
```

profile of v0, /device:TPU:0, one launch (start us, length us, event | category | flops | bytes accessed | tf_op | source)
XLA Modules:
  0.0 94.0 jit_solution(4073056862240279345)
XLA Ops:
  7.2 0.0 copy-start.1
  7.2 0.0 copy-start
  7.2 0.0 all-gather.2.cloned.1.call-start
  7.2 1.5 %fusion.5 = f32[512]{0:T(512)S(1)} fusion(bf16[1,512,768]{2,1,0:T(8,128)(2,1)} %param.6), kind=kLoop, calls=%fused_computation.13 | loop fusion | flops 1179136 | bytes 788480 | tf_op jit(solution)/shard_map/reduce_sum | solution.py:12
  8.8 2.2 %fusion.6 = bf16[512,768]{1,0:T(8,128)(2,1)} fusion(bf16[1,512,768]{2,1,0:T(8,128)(2,1)} %param.6, f32[512]{0:T(512)S(1)} %add_rsqrt_fusion.1), kind=kLoop, calls=%fused_computation.14 | loop fusion | flops 1179648 | bytes 1574912 | tf_op jit(solution)/shard_map/convert_element_type | solution.py:13
  11.0 0.0 all-gather.2.cloned.1.call-update
  11.0 1.0 %fusion.7 = f32[128]{0:T(128)S(1)} fusion(bf16[1,128,768]{2,1,0:T(8,128)(2,1)} %param.7), kind=kLoop, calls=%fused_computation.17 | loop fusion | flops 294784 | bytes 197120 | tf_op jit(solution)/shard_map/reduce_sum | solution.py:12
  12.1 0.0 copy-done
  12.1 0.7 fusion.2
  12.8 0.0 copy-done.1
  12.8 0.1 fusion.8
  12.9 10.6 %all_gather.6 = bf16[512,768]{1,0:T(8,128)(2,1)} all-gather(bf16[128,768]{1,0:T(8,128)(2,1)S(1)} %fusion.8), channel_id=1, replica_groups=mesh['slab'=2,'gal'=4,'qb'=4] {'gal'}, dimensions={0}, use_global_device_ids=true | all-gather | bytes 983040 | tf_op jit(solution)/shard_map/all_gather | solution.py:41
  23.5 2.3 %fusion.3 = bf16[2048,768]{1,0:T(8,128)(2,1)} fusion(bf16[2048,768]{1,0:T(8,128)(2,1)S(1)} %copy-done, f32[2048]{0:T(1024)S(1)} %add_rsqrt_fusion), kind=kLoop, calls=%fused_computation.7 | loop fusion | flops 4718592 | bytes 6299648 | tf_op jit(solution)/shard_map/convert_element_type | solution.py:13
  25.8 16.6 %all-gather.2.cloned.1.call-done = bf16[2048,768]{1,0:T(8,128)(2,1)} async-done(((bf16[512,768]{1,0:T(8,128)(2,1)}), bf16[2048,768]{1,0:T(8,128)(2,1)}) %all-gather.2.cloned.1.call-update) | async-done | bytes 3145744 | tf_op jit(solution)/shard_map/all_gather | solution.py:39
  42.4 16.3 %while.16 = (s32[]{:T(128)}, f32[2048]{0:T(1024)S(1)}, bf16[2048,768]{1,0:T(8,128)(2,1)}, bf16[2048,768]{1,0:T(8,128)(2,1)}, s32[]{:T(128)}, /*index=5*/s32[]{:T(128)}, s32[]{:T(128)}, s32[]{:T(128)}) while((s32[]{:T(128)}, f32[2048]{0:T(1024)S(1)}, bf16[2048,768]{1,0:T(8,128)(2,1)}, bf16[2048,768]{1,0:T(8,128)(2,1)}, s32[]{:T(128)}, ...), condition=%wide.region_5.0_spmd.clone, body=%wide.region_3.0_spmd.clone.sunk | while | flops 1613760512 | bytes 3965081 | solution.py:32
  42.4 4.1 %exponential_reduce_fusion.3 = f32[2048]{0:T(1024)S(1)} fusion(bf16[2048,768]{1,0:T(8,128)(2,1)} %get-tuple-element.182, bf16[2048,768]{1,0:T(8,128)(2,1)} %get-tuple-element.181, s32[]{:T(128)S(6)} %select_n.12), kind=kOutput, calls=%fused_computation.clone.1 | convolution fusion | flops 1613756416 | bytes 3940356 | tf_op jit(solution)/shard_map/while/body/eval_jaxpr/dot_general | solution.py:17
  46.5 4.0 %exponential_reduce_fusion.3 = f32[2048]{0:T(1024)S(1)} fusion(bf16[2048,768]{1,0:T(8,128)(2,1)} %get-tuple-element.182, bf16[2048,768]{1,0:T(8,128)(2,1)} %get-tuple-element.181, s32[]{:T(128)S(6)} %select_n.12), kind=kOutput, calls=%fused_computation.clone.1 | convolution fusion | flops 1613756416 | bytes 3940356 | tf_op jit(solution)/shard_map/while/body/eval_jaxpr/dot_general | solution.py:17
  50.6 4.0 %exponential_reduce_fusion.3 = f32[2048]{0:T(1024)S(1)} fusion(bf16[2048,768]{1,0:T(8,128)(2,1)} %get-tuple-element.182, bf16[2048,768]{1,0:T(8,128)(2,1)} %get-tuple-element.181, s32[]{:T(128)S(6)} %select_n.12), kind=kOutput, calls=%fused_computation.clone.1 | convolution fusion | flops 1613756416 | bytes 3940356 | tf_op jit(solution)/shard_map/while/body/eval_jaxpr/dot_general | solution.py:17
  54.6 4.0 %exponential_reduce_fusion.3 = f32[2048]{0:T(1024)S(1)} fusion(bf16[2048,768]{1,0:T(8,128)(2,1)} %get-tuple-element.182, bf16[2048,768]{1,0:T(8,128)(2,1)} %get-tuple-element.181, s32[]{:T(128)S(6)} %select_n.12), kind=kOutput, calls=%fused_computation.clone.1 | convolution fusion | flops 1613756416 | bytes 3940356 | tf_op jit(solution)/shard_map/while/body/eval_jaxpr/dot_general | solution.py:17
  58.7 11.8 %psum.14 = f32[2048]{0:T(1024)S(1)} all-reduce(f32[2048]{0:T(1024)S(1)} %get-tuple-element.112), channel_id=1, replica_groups=mesh['slab'=2,'gal'=4,'qb'=4] {'qb'}, use_global_device_ids=true, to_apply=%region_6.0 | all-reduce | flops 2048 | bytes 16384 | tf_op jit(solution)/shard_map/psum | solution.py:42
  70.5 0.0 copy-start.3
  70.6 5.9 %exponential_reduce_fusion.1 = (f32[512]{0:T(512)S(1)}, f32[512,2048]{1,0:T(8,128)}) fusion(f32[2048]{0:T(1024)S(1)} %log_add_fusion, bf16[512,768]{1,0:T(8,128)(2,1)S(1)} %copy-done.2, bf16[2048,768]{1,0:T(8,128)(2,1)} %get-tuple-element.188), kind=kOutput, calls=%fused_computation.8 | convolution fusion | flops 1614806528 | bytes 8136704 | tf_op jit(solution)/shard_map/dot_general | solution.py:46
  76.5 5.9 %psum.15 = f32[512]{0:T(512)S(1)} all-reduce(f32[512]{0:T(512)S(1)} %get-tuple-element.136), channel_id=1, replica_groups=mesh['slab'=2,'gal'=4,'qb'=4] {'gal'}, use_global_device_ids=true, to_apply=%region_8.0 | all-reduce | flops 512 | bytes 4096 | tf_op jit(solution)/shard_map/psum | solution.py:51
  82.4 4.8 %fusion.4 = f32[512,2048]{1,0:T(8,128)} fusion(f32[512,2048]{1,0:T(8,128)} %get-tuple-element.137, f32[512]{0:T(512)S(1)} %log.7, f32[2048]{0:T(1024)S(1)} %log_add_fusion), kind=kLoop, calls=%fused_computation.10 | loop fusion | flops 4194304 | bytes 8398848 | tf_op jit(solution)/shard_map/sub | solution.py:52
  (13 shorter events, 0.1 us)
Async XLA Ops:
  7.2 5.6 %copy-start.1 = (bf16[1,128,768]{2,1,0:T(8,128)(2,1)S(1)}, bf16[1,128,768]{2,1,0:T(8,128)(2,1)}, u32[]{:S(2)}) copy-start(bf16[1,128,768]{2,1,0:T(8,128)(2,1)} %param.7) | copy-start | bytes 589828
  7.2 4.9 %copy-start = (bf16[2048,768]{1,0:T(8,128)(2,1)S(1)}, bf16[2048,768]{1,0:T(8,128)(2,1)}, u32[]{:S(2)}) copy-start(bf16[2048,768]{1,0:T(8,128)(2,1)} %param.5) | copy-start | bytes 9437188
  7.2 35.2 %all-gather.2.cloned.1.call-start = ((), (), s32[]{:S(2)}) async-start(), calls=%async_computation | async-start | bytes 3932160 | tf_op jit(solution)/shard_map/all_gather | solution.py:39
  42.4 28.2 %copy-start.2 = (bf16[512,768]{1,0:T(8,128)(2,1)S(1)}, bf16[512,768]{1,0:T(8,128)(2,1)}, u32[]{:S(2)}) copy-start(bf16[512,768]{1,0:T(8,128)(2,1)} %all_gather.6) | copy-start | bytes 2359300
  70.5 11.9 %copy-start.3 = (f32[2048]{0:T(1024)}, f32[2048]{0:T(1024)S(1)}, u32[]{:S(2)}) copy-start(f32[2048]{0:T(1024)S(1)} %log_add_fusion) | copy-start | bytes 24580
Sparse Core Ops, SparseCore 0:
  11.1 31.2 all-gather.1
where the time goes:
time: 94.4 us; the launch traced here: 94 us
  blocking collectives  28.3 us (30%)
  matrix products  22.1 us (23%)
  waiting for transfers between devices  16.6 us (18%)
  between operations  14.1 us (15%)
  other arithmetic  12.7 us (13%)
    all_gather x1, waiting for transfers between devices, per_device(): bank_all = lax.all_gather(bank_local, 'gal', axis=0, tiled=True)  16.6 us
    dot_general x4, matrix products, column_terms(): lax.dot_general(bank_block, gallery_unit, (((1,), (1,)), ((), ())), prefe...  16.1 us
    psum x1, blocking collectives, per_device(): column_total = lax.psum(column_part, 'qb')  11.8 us
    all_gather x1, blocking collectives, per_device(): test_all = lax.all_gather(test_local, 'gal', axis=0, tiled=True)  10.6 us
    dot_general x1, matrix products, per_device(): lax.dot_general(test_all, gallery_unit, (((1,), (1,)), ((), ())), preferr...  5.95 us
    psum x1, blocking collectives, per_device(): row_total = lax.psum(row_part, 'gal')  5.9 us
    sub x1, other arithmetic, per_device(): logprob = logits - jnp.log(row_total)[:, None]  4.79 us
    convert_element_type x3, other arithmetic, unit_rows(): return scaled.astype(jnp.bfloat16)  4.59 us
  transfers between devices with their start and end apart: 1, of which 1 were waited for; matrix products, arithmetic and copies ran while one was open for 4% of the time, Pallas kernels for 0%

commit v1 on v0

--- a/solution.py
+++ b/solution.py
@@ -5,6 +5,28 @@
 from jax.sharding import PartitionSpec as P
 
 sharpness = 20.0
+
+
+def unit_fill(tile_in, array_dim):
+    tile_in = jnp.moveaxis(tile_in, 0, array_dim)
+    row_out = tile_in.shape
+    return tile_in.reshape(
+        *row_out[:array_dim], row_out[array_dim] * row_out[array_dim + 1], *row_out[array_dim + 2 :]
+    )
+
+
+def _deliver_set(my_tile, along_axis):
+    dev_n = jax.lax.axis_size(along_axis)
+    u1 = my_tile[None]
+    for m in range(dev_n.bit_length() - 1):
+        even = 1 << m
+        a_next = jax.lax.ppermute(
+            u1, along_axis, tuple(((dev_i, dev_i ^ even) for dev_i in range(dev_n)))
+        )
+        small = jnp.stack([u1, a_next])
+        long_array = jax.lax.axis_index(along_axis) >> m & 1
+        u1 = jnp.where(long_array == 0, small, small[::-1]).reshape(-1, *my_tile.shape)
+    return u1
 
 
 def unit_rows(values):
@@ -38,7 +60,7 @@
     test_local = unit_rows(test_queries[0])
     bank_all = lax.all_gather(bank_local, "gal", axis=0, tiled=True)
     column_part = bank_columns(bank_all, gallery_unit)
-    test_all = lax.all_gather(test_local, "gal", axis=0, tiled=True)
+    test_all = unit_fill(_deliver_set(test_local, "gal"), 0)
     column_total = lax.psum(column_part, "qb")
     normalizer = sharpness + jnp.log(column_total)
     bank_count = querybank.shape[1] * lax.axis_size("gal") * lax.axis_size("qb")

time: 94.4 us -> 98.5 us (1.043)
  blocking collectives: 28.3 us -> 18 us
  waiting for transfers between devices: 16.6 us -> 25.7 us
  starting transfers between devices: 0.04 us -> 3.2 us
  other arithmetic: 12.7 us -> 15 us
    ppermute x0 -> x2, waiting for transfers between devices: none -> 12.5 us  [_deliver_set(): jax.lax.ppermute(u1, along_axis, tuple(((dev_i, dev_i ^ even) for dev_i i...]
    all_gather x1 -> x0, blocking collectives: 10.6 us -> none  [per_device(): test_all = lax.all_gather(test_local, 'gal', axis=0, tiled=True)]
    all_gather x1, waiting for transfers between devices: 16.6 us -> 13.1 us  [per_device(): bank_all = lax.all_gather(bank_local, 'gal', axis=0, tiled=True)]
    ppermute x0 -> x2, starting transfers between devices: none -> 3.16 us  [_deliver_set(): jax.lax.ppermute(u1, along_axis, tuple(((dev_i, dev_i ^ even) for dev_i i...]
    convert_element_type x3 -> x4, other arithmetic: 4.59 us -> 6.54 us  [unit_rows(): return scaled.astype(jnp.bfloat16)]
  transfers between devices with their start and end apart: 1 -> 3, of which waited for: 1 -> 2; matrix products, arithmetic and copies ran while one was open for 4% -> 7% of each run, Pallas kernels for 0% -> 0%
where the time goes in v1:
time: 98.5 us; the launch traced here: 98.1 us
  waiting for transfers between devices  25.7 us (26%)
  matrix products  22 us (22%)
  blocking collectives  18 us (18%)
  other arithmetic  15 us (15%)
  between operations  14.1 us (14%)
  starting transfers between devices  3.2 us (3%)
    dot_general x4, matrix products, column_terms(): lax.dot_general(bank_block, gallery_unit, (((1,), (1,)), ((), ())), prefe...  16.1 us
    all_gather x1, waiting for transfers between devices, per_device(): bank_all = lax.all_gather(bank_local, 'gal', axis=0, tiled=True)  13.1 us
    ppermute x2, waiting for transfers between devices, _deliver_set(): jax.lax.ppermute(u1, along_axis, tuple(((dev_i, dev_i ^ even) for dev_i i...  12.5 us
    psum x1, blocking collectives, per_device(): column_total = lax.psum(column_part, 'qb')  12.3 us
    convert_element_type x4, other arithmetic, unit_rows(): return scaled.astype(jnp.bfloat16)  6.54 us
    dot_general x1, matrix products, per_device(): lax.dot_general(test_all, gallery_unit, (((1,), (1,)), ((), ())), preferr...  5.95 us
    psum x1, blocking collectives, per_device(): row_total = lax.psum(row_part, 'gal')  5.63 us
    sub x1, other arithmetic, per_device(): logprob = logits - jnp.log(row_total)[:, None]  4.79 us
  transfers between devices with their start and end apart: 3, of which 2 were waited for; matrix products, arithmetic and copies ran while one was open for 7% of the time, Pallas kernels for 0%

profile of v1, /device:TPU:0, one launch (start us, length us, event | category | flops | bytes accessed | tf_op | source)
XLA Modules:
  0.0 98.1 jit_solution(3659482057743307043)
XLA Ops:
  7.2 0.0 all-gather.2.cloned.1.call-start
  7.2 1.5 %fusion.5 = f32[512]{0:T(512)S(1)} fusion(bf16[1,512,768]{2,1,0:T(8,128)(2,1)} %param.6), kind=kLoop, calls=%fused_computation.13 | loop fusion | flops 1179136 | bytes 788480 | tf_op jit(solution)/shard_map/reduce_sum | solution.py:34
  8.7 2.2 %fusion.6 = bf16[512,768]{1,0:T(8,128)(2,1)} fusion(bf16[1,512,768]{2,1,0:T(8,128)(2,1)} %param.6, f32[512]{0:T(512)S(1)} %add_rsqrt_fusion.1), kind=kLoop, calls=%fused_computation.14 | loop fusion | flops 1179648 | bytes 1574912 | tf_op jit(solution)/shard_map/convert_element_type | solution.py:35
  11.0 1.0 %fusion.9 = f32[128]{0:T(128)S(1)} fusion(bf16[1,128,768]{2,1,0:T(8,128)(2,1)} %param.7), kind=kLoop, calls=%fused_computation.23 | loop fusion | flops 294784 | bytes 197120 | tf_op jit(solution)/shard_map/reduce_sum | solution.py:34
  12.0 1.0 %fusion.10 = bf16[1,128,768]{2,1,0:T(8,128)(2,1)S(1)} fusion(bf16[1,128,768]{2,1,0:T(8,128)(2,1)} %param.7, f32[128]{0:T(128)S(1)} %add_rsqrt_fusion.2), kind=kLoop, calls=%fused_computation.24 | loop fusion | flops 294912 | bytes 393728 | tf_op jit(solution)/shard_map/convert_element_type | solution.py:35
  13.1 0.6 collective-permute-start
  13.6 1.0 %fusion.8 = bf16[1,1,128,768]{3,2,1,0:T(8,128)(2,1)S(1)} fusion(bf16[1,128,768]{2,1,0:T(8,128)(2,1)} %param.7, f32[128]{0:T(128)S(1)} %add_rsqrt_fusion.2), kind=kLoop, calls=%fused_computation.22 | loop fusion | flops 294912 | bytes 393728 | tf_op jit(solution)/shard_map/convert_element_type | solution.py:35
  14.7 0.7 fusion.2
  15.4 0.1 fusion.12
  15.5 2.6 %collective-permute-start.1 = (bf16[2,128,768]{2,1,0:T(8,128)(2,1)S(1)}, bf16[2,128,768]{2,1,0:T(8,128)(2,1)S(1)}, u32[]{:S(2)}, u32[]{:S(2)}) collective-permute-start(bf16[2,128,768]{2,1,0:T(8,128)(2,1)S(1)} %get-tuple-element.137), channel_id=1, source_target_pairs={{0,8},{4,12},{8,0},{12,4},{1,9},{5,13},{9,1},{13,5},{2,10},{6,14},... | collective-permute-start | bytes 1179656 | tf_op jit(solution)/shard_map/ppermute | solution.py:23
  18.1 2.3 %fusion.3 = bf16[2048,768]{1,0:T(8,128)(2,1)} fusion(bf16[2048,768]{1,0:T(8,128)(2,1)S(1)} %copy-done, f32[2048]{0:T(1024)S(1)} %add_rsqrt_fusion), kind=kLoop, calls=%fused_computation.7 | loop fusion | flops 4718592 | bytes 6299648 | tf_op jit(solution)/shard_map/convert_element_type | solution.py:35
  20.4 12.5 %collective-permute-done.1 = bf16[2,128,768]{2,1,0:T(8,128)(2,1)S(1)} collective-permute-done((bf16[2,128,768]{2,1,0:T(8,128)(2,1)S(1)}, bf16[2,128,768]{2,1,0:T(8,128)(2,1)S(1)}, u32[]{:S(2)}, u32[]{:S(2)}) %collective-permute-start.1) | collective-permute-done | bytes 393248 | tf_op jit(solution)/shard_map/ppermute | solution.py:23
  32.9 0.1 pad_maximum_fusion
  33.0 0.1 reverse_select_fusion
  33.2 13.1 %all-gather.2.cloned.1.call-done = bf16[2048,768]{1,0:T(8,128)(2,1)} async-done(((bf16[512,768]{1,0:T(8,128)(2,1)}), bf16[2048,768]{1,0:T(8,128)(2,1)}) %all-gather.2.cloned.1.call-update) | async-done | bytes 3145744 | tf_op jit(solution)/shard_map/all_gather | solution.py:61
  46.3 16.2 %while.16 = (s32[]{:T(128)}, f32[2048]{0:T(1024)S(1)}, bf16[2048,768]{1,0:T(8,128)(2,1)}, bf16[2048,768]{1,0:T(8,128)(2,1)}, s32[]{:T(128)}, /*index=5*/s32[]{:T(128)}, s32[]{:T(128)}, s32[]{:T(128)}) while((s32[]{:T(128)}, f32[2048]{0:T(1024)S(1)}, bf16[2048,768]{1,0:T(8,128)(2,1)}, bf16[2048,768]{1,0:T(8,128)(2,1)}, s32[]{:T(128)}, ...), condition=%wide.region_5.0_spmd.clone, body=%wide.region_3.0_spmd.clone.sunk | while | flops 1613760512 | bytes 3965081 | solution.py:54
  46.3 4.0 %exponential_reduce_fusion.3 = f32[2048]{0:T(1024)S(1)} fusion(bf16[2048,768]{1,0:T(8,128)(2,1)} %get-tuple-element.184, bf16[2048,768]{1,0:T(8,128)(2,1)} %get-tuple-element.183, s32[]{:T(128)S(6)} %select_n.44), kind=kOutput, calls=%fused_computation.clone.1 | convolution fusion | flops 1613756416 | bytes 3940356 | tf_op jit(solution)/shard_map/while/body/eval_jaxpr/dot_general | solution.py:39
  50.4 4.0 %exponential_reduce_fusion.3 = f32[2048]{0:T(1024)S(1)} fusion(bf16[2048,768]{1,0:T(8,128)(2,1)} %get-tuple-element.184, bf16[2048,768]{1,0:T(8,128)(2,1)} %get-tuple-element.183, s32[]{:T(128)S(6)} %select_n.44), kind=kOutput, calls=%fused_computation.clone.1 | convolution fusion | flops 1613756416 | bytes 3940356 | tf_op jit(solution)/shard_map/while/body/eval_jaxpr/dot_general | solution.py:39
  54.4 4.0 %exponential_reduce_fusion.3 = f32[2048]{0:T(1024)S(1)} fusion(bf16[2048,768]{1,0:T(8,128)(2,1)} %get-tuple-element.184, bf16[2048,768]{1,0:T(8,128)(2,1)} %get-tuple-element.183, s32[]{:T(128)S(6)} %select_n.44), kind=kOutput, calls=%fused_computation.clone.1 | convolution fusion | flops 1613756416 | bytes 3940356 | tf_op jit(solution)/shard_map/while/body/eval_jaxpr/dot_general | solution.py:39
  58.5 4.0 %exponential_reduce_fusion.3 = f32[2048]{0:T(1024)S(1)} fusion(bf16[2048,768]{1,0:T(8,128)(2,1)} %get-tuple-element.184, bf16[2048,768]{1,0:T(8,128)(2,1)} %get-tuple-element.183, s32[]{:T(128)S(6)} %select_n.44), kind=kOutput, calls=%fused_computation.clone.1 | convolution fusion | flops 1613756416 | bytes 3940356 | tf_op jit(solution)/shard_map/while/body/eval_jaxpr/dot_general | solution.py:39
  62.5 12.3 %psum.14 = f32[2048]{0:T(1024)S(1)} all-reduce(f32[2048]{0:T(1024)S(1)} %get-tuple-element.112), channel_id=1, replica_groups=mesh['slab'=2,'gal'=4,'qb'=4] {'qb'}, use_global_device_ids=true, to_apply=%region_6.7 | all-reduce | flops 2048 | bytes 16384 | tf_op jit(solution)/shard_map/psum | solution.py:64
  74.9 6.0 %exponential_reduce_fusion.1 = (f32[512]{0:T(512)S(1)}, f32[512,2048]{1,0:T(8,128)}) fusion(f32[2048]{0:T(1024)S(1)} %log_add_fusion, bf16[512,768]{1,0:T(8,128)(2,1)S(1)} %bitcast.22, bf16[2048,768]{1,0:T(8,128)(2,1)} %get-tuple-element.190), kind=kOutput, calls=%fused_computation.8 | convolution fusion | flops 1614806528 | bytes 8136704 | tf_op jit(solution)/shard_map/dot_general | solution.py:68
  80.9 5.6 %psum.15 = f32[512]{0:T(512)S(1)} all-reduce(f32[512]{0:T(512)S(1)} %get-tuple-element.138), channel_id=1, replica_groups=mesh['slab'=2,'gal'=4,'qb'=4] {'gal'}, use_global_device_ids=true, to_apply=%region_8.9 | all-reduce | flops 512 | bytes 4096 | tf_op jit(solution)/shard_map/psum | solution.py:73
  86.5 4.8 %fusion.4 = f32[512,2048]{1,0:T(8,128)} fusion(f32[512,2048]{1,0:T(8,128)} %get-tuple-element.139, f32[512]{0:T(512)S(1)} %log.7, f32[2048]{0:T(1024)S(1)} %log_add_fusion), kind=kLoop, calls=%fused_computation.10 | loop fusion | flops 4194304 | bytes 8398848 | tf_op jit(solution)/shard_map/sub | solution.py:74
  (17 shorter events, 0.1 us)
Async XLA Ops:
  7.2 7.5 %copy-start = (bf16[2048,768]{1,0:T(8,128)(2,1)S(1)}, bf16[2048,768]{1,0:T(8,128)(2,1)}, u32[]{:S(2)}) copy-start(bf16[2048,768]{1,0:T(8,128)(2,1)} %param.5) | copy-start | bytes 9437188
  7.2 39.1 %all-gather.2.cloned.1.call-start = ((), (), s32[]{:S(2)}) async-start(), calls=%async_computation | async-start | bytes 3932160 | tf_op jit(solution)/shard_map/all_gather | solution.py:61
  13.1 2.3 %collective-permute-start = (bf16[1,128,768]{2,1,0:T(8,128)(2,1)S(1)}, bf16[1,128,768]{2,1,0:T(8,128)(2,1)S(1)}, u32[]{:S(2)}, u32[]{:S(2)}) collective-permute-start(bf16[1,128,768]{2,1,0:T(8,128)(2,1)S(1)} %fusion.10), channel_id=1, source_target_pairs={{0,4},{4,0},{8,12},{12,8},{1,5},{5,1},{9,13},{13,9},{2,6},{6,2},{1... | collective-permute-start | bytes 589832 | tf_op jit(solution)/shard_map/ppermute | solution.py:23
  15.5 17.4 %collective-permute-start.1 = (bf16[2,128,768]{2,1,0:T(8,128)(2,1)S(1)}, bf16[2,128,768]{2,1,0:T(8,128)(2,1)S(1)}, u32[]{:S(2)}, u32[]{:S(2)}) collective-permute-start(bf16[2,128,768]{2,1,0:T(8,128)(2,1)S(1)} %get-tuple-element.137), channel_id=1, source_target_pairs={{0,8},{4,12},{8,0},{12,4},{1,9},{5,13},{9,1},{13,5},{2,10},{6,14},... | collective-permute-start | bytes 1179656 | tf_op jit(solution)/shard_map/ppermute | solution.py:23
  74.9 11.6 %copy-start.1 = (f32[2048]{0:T(1024)}, f32[2048]{0:T(1024)S(1)}, u32[]{:S(2)}) copy-start(f32[2048]{0:T(1024)S(1)} %log_add_fusion) | copy-start | bytes 24580
Sparse Core Ops, SparseCore 0:
  11.1 35.1 all-gather.1
